TPU v7x, 32 devices: a whole 2x2x4 slice. The times are simulated.
32 devices in a mesh: grp: 2 (over x), tok: 16 (over z, y, core).
Axes of the slice: x: 2, y: 2, z: 4, core: 2. Of those that a mesh axis runs over, the one named last changes fastest.
Arguments:
- keys: bfloat16 [4096, 1024], P(('grp', 'tok')), parts along dimension 0, may hold values from -6 to 6
- values: bfloat16 [4096, 1024], P(('grp', 'tok')), parts along dimension 0, may hold values from -6 to 6
- queries: bfloat16 [4096, 1024], P(('grp', 'tok')), parts along dimension 0, may hold values from -6 to 6
- rates: float32 [2, 4096], P(None, ('grp', 'tok')), parts along dimension 1, may hold values from 0.3 to 3
- fast_weights: bfloat16 [2, 3, 512, 512], replicated, may hold values from -0.25 to 0.25
Outputs:
- readout: bfloat16 [4096, 1024], P(('grp', 'tok')), parts along dimension 0
- new_weights: bfloat16 [4, 3, 512, 512], P('grp'), parts along dimension 0
There are 2 independent parts, one for each index of `grp`. A program takes and returns all parts, laid end to end along the dimension named above; an argument that names none is the same for every part. Nothing has to cross between parts.
All inputs are finite; a program needn't handle non-finite values.
Results may differ from a plain program's by a relative error of at most 0.017.
Values may be sent and summed in bfloat16 or wider, within the bound.
A program may use at most 64 MiB of HBM per device.

v0:
```python
import jax
import jax.numpy as jnp
from jax import lax
from jax.sharding import PartitionSpec as P

DH = 512
HEADS = 2
NS_STEPS = 2


def swiglu_grads(key_rows, value_rows, rate_col, gate_w, up_w, down_w):
    gate = jnp.dot(key_rows, gate_w, preferred_element_type=jnp.float32)
    upper = jnp.dot(key_rows, up_w, preferred_element_type=jnp.float32)
    sigma = jax.nn.sigmoid(gate)
    silu_gate = gate * sigma
    hidden = (silu_gate * upper).astype(jnp.bfloat16)
    outer = (-rate_col[:, None] * value_rows.astype(jnp.float32)).astype(jnp.bfloat16)
    back = jnp.dot(outer, down_w.T, preferred_element_type=jnp.float32)
    d_gate = (back * upper * sigma * (1.0 + gate * (1.0 - sigma))).astype(jnp.bfloat16)
    d_upper = (back * silu_gate).astype(jnp.bfloat16)
    grad_gate = jnp.dot(key_rows.T, d_gate, preferred_element_type=jnp.float32)
    grad_upper = jnp.dot(key_rows.T, d_upper, preferred_element_type=jnp.float32)
    grad_down = jnp.dot(hidden.T, outer, preferred_element_type=jnp.float32)
    return jnp.stack([grad_gate, grad_upper, grad_down])


def newton_schulz(matrix):
    wide = matrix.astype(jnp.float32)
    iterate = (wide / (jnp.sqrt(jnp.sum(wide * wide)) + 1e-07)).astype(jnp.bfloat16)
    for step in range(NS_STEPS):
        gram = jnp.dot(iterate, iterate.T, preferred_element_type=jnp.float32).astype(jnp.bfloat16)
        square = jnp.dot(gram, gram, preferred_element_type=jnp.float32)
        mixed = (-4.775 * gram.astype(jnp.float32) + 2.0315 * square).astype(jnp.bfloat16)
        iterate = (
            3.4445 * iterate.astype(jnp.float32)
            + jnp.dot(mixed, iterate, preferred_element_type=jnp.float32)
        ).astype(jnp.bfloat16)
    return iterate


def renormed(weight, update):
    old = weight.astype(jnp.float32)
    fresh = old - update.astype(jnp.float32)
    scale = jnp.sqrt(
        (jnp.mean(old * old, axis=1, keepdims=True) + 1e-06)
        / (jnp.mean(fresh * fresh, axis=1, keepdims=True) + 1e-06)
    )
    return (fresh * scale).astype(jnp.bfloat16)


def apply_fast(query_rows, gate_w, up_w, down_w):
    gate = jnp.dot(query_rows, gate_w, preferred_element_type=jnp.float32)
    upper = jnp.dot(query_rows, up_w, preferred_element_type=jnp.float32)
    hidden = (jax.nn.silu(gate) * upper).astype(jnp.bfloat16)
    return jnp.dot(hidden, down_w, preferred_element_type=jnp.float32).astype(jnp.bfloat16)


def summed_grads(partial_value):
    total = lax.psum(partial_value, "tok")
    return total.astype(jnp.bfloat16)


def body(keys, values, queries, rates, fast_weights):
    width = fast_weights.shape[2]
    count = 3 * HEADS
    rounded_all = []
    for head in range(HEADS):
        cols = slice(head * DH, (head + 1) * DH)
        partial_value = swiglu_grads(
            keys[:, cols],
            values[:, cols],
            rates[head],
            fast_weights[head, 0],
            fast_weights[head, 1],
            fast_weights[head, 2],
        )
        rounded_all.append(summed_grads(partial_value))
    stacked = jnp.concatenate(rounded_all, axis=0)
    old_all = fast_weights.reshape(count, width, width)
    fresh_all = [
        renormed(old_all[matrix], newton_schulz(stacked[matrix])) for matrix in range(count)
    ]
    outputs = []
    for head in range(HEADS):
        cols = slice(head * DH, (head + 1) * DH)
        outputs.append(
            apply_fast(
                queries[:, cols],
                fresh_all[3 * head],
                fresh_all[3 * head + 1],
                fresh_all[3 * head + 2],
            )
        )
    new_weights = jnp.stack(fresh_all).reshape(HEADS, 3, width, width)
    return (jnp.concatenate(outputs, axis=1), new_weights)


def solution(mesh):
    return jax.shard_map(
        body,
        mesh=mesh,
        in_specs=(
            P(("grp", "tok"), None),
            P(("grp", "tok"), None),
            P(("grp", "tok"), None),
            P(None, ("grp", "tok")),
            P(),
        ),
        out_specs=(P(("grp", "tok"), None), P("grp", None, None, None)),
        check_vma=False,
    )
```

profile of v0, /device:TPU:0, one launch (start us, length us, event | category | flops | bytes accessed | tf_op | source)
XLA Modules:
  0.0 251.6 jit_solution(15024841520664925883)
XLA Ops:
  0.7 0.9 negate_bitcast_fusion.1
  1.5 1.6 fusion.100
  3.1 1.3 fusion.94
  4.4 1.4 fusion.104
  5.9 1.4 fusion.98
  7.8 0.4 convolution_bitcast_fusion
  8.2 0.4 convolution_bitcast_fusion.2
  8.9 2.0 pad_maximum_fusion.1
  10.9 0.4 convolution_bitcast_fusion.3
  11.3 0.4 convolution_bitcast_fusion.5
  12.0 2.0 pad_maximum_fusion
  14.0 140.5 %all-reduce.2 = (bf16[3,512,512]{1,2,0:T(8,128)(2,1)}, bf16[3,512,512]{1,2,0:T(8,128)(2,1)}) all-reduce(f32[3,512,512]{1,2,0:T(8,128)} %pad_maximum_fusion.1, f32[3,512,512]{1,2,0:T(8,128)} %pad_maximum_fusion), channel_id=1, replica_groups=mesh['grp'=2,'tok'=16] {'tok'}, use_global_device_ids=true, to_apply=%region_10.0 | all-reduce | flops 1572864 | bytes 9437184 | tf_op jit(solution)/shard_map/psum | solution.py:59
  154.5 3.1 %fusion.50 = (f32[]{:T(128)}, f32[]{:T(128)}, f32[]{:T(128)}, f32[]{:T(128)}, f32[]{:T(128)}, /*index=5*/f32[]{:T(128)}) fusion(bf16[3,512,512]{1,2,0:T(8,128)(2,1)} %get-tuple-element.17, bf16[3,512,512]{1,2,0:T(8,128)(2,1)} %get-tuple-element.16), kind=kLoop, calls=%fused_computation.124 | loop fusion | flops 4718586 | bytes 3145752 | tf_op jit(solution)/shard_map/reduce_sum | solution.py:29
  161.7 2.6 %convolution_convert_fusion.7 = bf16[512,512]{1,0:T(8,128)(2,1)} fusion(f32[]{:T(128)S(6)} %add.226, bf16[3,512,512]{1,2,0:T(8,128)(2,1)} %get-tuple-element.17), kind=kOutput, calls=%fused_computation.87 | convolution fusion | flops 269484032 | bytes 1048580 | tf_op jit(solution)/shard_map/dot_general | solution.py:31
  164.3 3.5 %fusion.30 = bf16[512,512]{0,1:T(8,128)(2,1)} fusion(bf16[512,512]{1,0:T(8,128)(2,1)} %convolution_convert_fusion.7, f32[]{:T(128)S(6)} %add.226, bf16[3,512,512]{1,2,0:T(8,128)(2,1)} %get-tuple-element.17), kind=kOutput, calls=%fused_computation.98 | convolution fusion | flops 540803072 | bytes 3146752 | tf_op jit(solution)/shard_map/dot_general | solution.py:36
  167.8 2.5 convolution_convert_fusion.6
  170.3 2.5 convolution_convert_fusion.9
  172.8 3.5 %fusion.27 = bf16[512,512]{0,1:T(8,128)(2,1)} fusion(bf16[512,512]{1,0:T(8,128)(2,1)} %convolution_convert_fusion.9, f32[]{:T(128)S(6)} %add.219, bf16[3,512,512]{1,2,0:T(8,128)(2,1)} %get-tuple-element.17), kind=kOutput, calls=%fused_computation.95 | convolution fusion | flops 540803072 | bytes 3146752 | tf_op jit(solution)/shard_map/dot_general | solution.py:36
  176.2 2.5 convolution_convert_fusion.8
  178.7 2.5 convolution_convert_fusion.11
  181.2 3.5 %fusion.24 = bf16[512,512]{0,1:T(8,128)(2,1)} fusion(bf16[512,512]{1,0:T(8,128)(2,1)} %convolution_convert_fusion.11, f32[]{:T(128)S(6)} %add.211, bf16[3,512,512]{1,2,0:T(8,128)(2,1)} %get-tuple-element.17), kind=kOutput, calls=%fused_computation.92 | convolution fusion | flops 540803072 | bytes 3146752 | tf_op jit(solution)/shard_map/dot_general | solution.py:36
  184.7 2.5 convolution_convert_fusion.10
  187.2 2.5 convolution_convert_fusion.5
  189.6 3.5 %fusion.33 = bf16[512,512]{0,1:T(8,128)(2,1)} fusion(bf16[512,512]{1,0:T(8,128)(2,1)} %convolution_convert_fusion.5, f32[]{:T(128)S(6)} %add.235, bf16[3,512,512]{1,2,0:T(8,128)(2,1)} %get-tuple-element.16), kind=kOutput, calls=%fused_computation.101 | convolution fusion | flops 540803072 | bytes 3146752 | tf_op jit(solution)/shard_map/dot_general | solution.py:36
  193.1 2.5 convolution_convert_fusion.4
  195.6 2.5 convolution_convert_fusion.3
  198.1 3.6 %fusion.36 = bf16[512,512]{0,1:T(8,128)(2,1)} fusion(bf16[512,512]{1,0:T(8,128)(2,1)} %convolution_convert_fusion.3, f32[]{:T(128)S(6)} %add.243, bf16[3,512,512]{1,2,0:T(8,128)(2,1)} %get-tuple-element.16), kind=kOutput, calls=%fused_computation.104 | convolution fusion | flops 540803072 | bytes 3146752 | tf_op jit(solution)/shard_map/dot_general | solution.py:36
  201.7 2.6 %convolution_convert_fusion.2 = bf16[512,512]{1,0:T(8,128)(2,1)} fusion(bf16[512,512]{0,1:T(8,128)(2,1)} %fusion.36), kind=kOutput, calls=%fused_computation.82 | convolution fusion | flops 268697600 | bytes 1048576 | tf_op jit(solution)/shard_map/dot_general | solution.py:31
  204.3 2.5 convolution_convert_fusion.1
  206.7 3.4 %fusion.39 = bf16[512,512]{0,1:T(8,128)(2,1)} fusion(bf16[512,512]{1,0:T(8,128)(2,1)} %convolution_convert_fusion.1, f32[]{:T(128)S(6)} %add.250, bf16[3,512,512]{1,2,0:T(8,128)(2,1)} %get-tuple-element.16), kind=kOutput, calls=%fused_computation.107 | convolution fusion | flops 540803072 | bytes 3146752 | tf_op jit(solution)/shard_map/dot_general | solution.py:36
  210.2 2.5 convolution_convert_fusion
  212.6 2.8 %copy.7 = bf16[2,3,512,512]{2,3,1,0:T(8,128)(2,1)} copy(bf16[2,3,512,512]{3,2,1,0:T(8,128)(2,1)S(1)} %copy-done) | data formatting | bytes 6291456 | tf_op args[4]
  215.4 3.8 %multiply_reduce_fusion = (f32[512]{0:T(512)S(1)}, f32[512,512]{0,1:T(8,128)}) fusion(bf16[512,512]{0,1:T(8,128)(2,1)} %fusion.39, bf16[512,512]{1,0:T(8,128)(2,1)} %convolution_convert_fusion, bf16[6,512,512]{1,2,0:T(8,128)(2,1)} %bitcast.202), kind=kOutput, calls=%fused_computation.139 | convolution fusion | flops 540540416 | bytes 4196352 | tf_op jit(solution)/shard_map/dot_general | solution.py:36
  219.2 3.6 %multiply_reduce_fusion.1 = (f32[512]{0:T(512)S(1)}, f32[512,512]{0,1:T(8,128)}) fusion(bf16[512,512]{0,1:T(8,128)(2,1)} %fusion.36, bf16[512,512]{1,0:T(8,128)(2,1)} %convolution_convert_fusion.2, bf16[6,512,512]{1,2,0:T(8,128)(2,1)S(1)} %bitcast.203), kind=kOutput, calls=%fused_computation.145 | convolution fusion | flops 540540416 | bytes 4196352 | tf_op jit(solution)/shard_map/dot_general | solution.py:36
  222.8 3.6 %multiply_reduce_fusion.2 = (f32[512]{0:T(512)S(1)}, f32[512,512]{0,1:T(8,128)}) fusion(bf16[512,512]{0,1:T(8,128)(2,1)} %fusion.33, bf16[512,512]{1,0:T(8,128)(2,1)} %convolution_convert_fusion.4, bf16[6,512,512]{1,2,0:T(8,128)(2,1)S(1)} %bitcast.204), kind=kOutput, calls=%fused_computation.151 | convolution fusion | flops 540540416 | bytes 4196352 | tf_op jit(solution)/shard_map/dot_general | solution.py:36
  226.4 3.6 %multiply_reduce_fusion.3 = (f32[512]{0:T(512)S(1)}, f32[512,512]{0,1:T(8,128)}) fusion(bf16[512,512]{0,1:T(8,128)(2,1)} %fusion.30, bf16[512,512]{1,0:T(8,128)(2,1)} %convolution_convert_fusion.6, bf16[6,512,512]{1,2,0:T(8,128)(2,1)S(1)} %bitcast.205), kind=kOutput, calls=%fused_computation.157 | convolution fusion | flops 540540416 | bytes 4196352 | tf_op jit(solution)/shard_map/dot_general | solution.py:36
  230.0 3.7 %multiply_reduce_fusion.4 = (f32[512]{0:T(512)S(1)}, f32[512,512]{0,1:T(8,128)}) fusion(bf16[512,512]{0,1:T(8,128)(2,1)} %fusion.27, bf16[512,512]{1,0:T(8,128)(2,1)} %convolution_convert_fusion.8, bf16[6,512,512]{1,2,0:T(8,128)(2,1)S(1)} %bitcast.206), kind=kOutput, calls=%fused_computation.163 | convolution fusion | flops 540540416 | bytes 4196352 | tf_op jit(solution)/shard_map/dot_general | solution.py:36
  233.7 3.8 %multiply_reduce_fusion.5 = (f32[512]{0:T(512)S(1)}, f32[512,512]{0,1:T(8,128)}) fusion(bf16[512,512]{0,1:T(8,128)(2,1)} %fusion.24, bf16[512,512]{1,0:T(8,128)(2,1)} %convolution_convert_fusion.10, bf16[6,512,512]{1,2,0:T(8,128)(2,1)S(1)} %bitcast.207), kind=kOutput, calls=%fused_computation.169 | convolution fusion | flops 540540416 | bytes 4196352 | tf_op jit(solution)/shard_map/dot_general | solution.py:36
  237.5 0.6 fusion.60
  238.2 0.6 fusion.171
  238.8 0.6 fusion.172
  239.8 2.1 convolution_convert_fusion.12
  241.9 1.2 convolution_bitcast_fusion.9
  243.2 1.4 convolution_convert_fusion.13
  244.7 0.7 pad_maximum_fusion.2
  245.4 1.4 bitcast_dynamic-update-slice_fusion.5
  246.8 1.4 bitcast_dynamic-update-slice_fusion.4
  248.8 2.8 %copy.12 = bf16[2,3,512,512]{3,2,1,0:T(8,128)(2,1)} copy(bf16[2,3,512,512]{2,3,1,0:T(8,128)(2,1)S(1)} %bitcast.209) | data formatting | bytes 6291456
  (41 shorter events, 2.0 us)
Async XLA Ops:
  0.6 6.7 %copy-start.10 = (bf16[128,1024]{1,0:T(8,128)(2,1)S(1)}, bf16[128,1024]{1,0:T(8,128)(2,1)}, u32[]{:S(2)}) copy-start(bf16[128,1024]{1,0:T(8,128)(2,1)} %param.5) | copy-start | bytes 786436
  0.6 6.7 %copy-start = (bf16[2,3,512,512]{3,2,1,0:T(8,128)(2,1)S(1)}, bf16[2,3,512,512]{3,2,1,0:T(8,128)(2,1)}, u32[]{:S(2)}) copy-start(bf16[2,3,512,512]{3,2,1,0:T(8,128)(2,1)} %param.9) | copy-start | bytes 9437188
  0.7 7.1 %copy-start.11 = (bf16[128,1024]{1,0:T(8,128)(2,1)S(1)}, bf16[128,1024]{1,0:T(8,128)(2,1)}, u32[]{:S(2)}) copy-start(bf16[128,1024]{1,0:T(8,128)(2,1)} %param.6) | copy-start | bytes 786436
  215.4 3.8 %copy-start.1 = (bf16[2,3,512,512]{2,3,1,0:T(8,128)(2,1)S(1)}, bf16[2,3,512,512]{2,3,1,0:T(8,128)(2,1)}, u32[]{:S(2)}) copy-start(bf16[2,3,512,512]{2,3,1,0:T(8,128)(2,1)} %copy.7) | copy-start | bytes 9437188
  237.5 2.0 copy-start.7
  237.5 2.0 copy-start.12
  238.1 3.8 %copy-start.9 = (f32[512,512]{0,1:T(8,128)S(1)}, f32[512,512]{0,1:T(8,128)}, u32[]{:S(2)}) copy-start(f32[512,512]{0,1:T(8,128)} %get-tuple-element.27) | copy-start | bytes 3145732
  238.1 5.0 %copy-start.4 = (f32[512,512]{0,1:T(8,128)S(1)}, f32[512,512]{0,1:T(8,128)}, u32[]{:S(2)}) copy-start(f32[512,512]{0,1:T(8,128)} %get-tuple-element.31) | copy-start | bytes 3145732
  238.1 5.0 %copy-start.6 = (f32[512,512]{0,1:T(8,128)S(1)}, f32[512,512]{0,1:T(8,128)}, u32[]{:S(2)}) copy-start(f32[512,512]{0,1:T(8,128)} %get-tuple-element.29) | copy-start | bytes 3145732
  244.6 3.7 %copy-start.5 = (f32[512,512]{0,1:T(8,128)S(1)}, f32[512,512]{0,1:T(8,128)}, u32[]{:S(2)}) copy-start(f32[512,512]{0,1:T(8,128)} %get-tuple-element.31) | copy-start | bytes 3145732
  244.6 3.7 %copy-start.13 = (f32[512]{0:T(512)S(1)}, f32[512]{0:T(512)}, u32[]{:S(2)}) copy-start(f32[512]{0:T(512)} %fusion.172) | copy-start | bytes 6148
  244.6 3.8 %copy-start.8 = (f32[512,512]{0,1:T(8,128)S(1)}, f32[512,512]{0,1:T(8,128)}, u32[]{:S(2)}) copy-start(f32[512,512]{0,1:T(8,128)} %get-tuple-element.21) | copy-start | bytes 3145732
  245.4 3.2 %copy-start.3 = (f32[512,512]{0,1:T(8,128)S(1)}, f32[512,512]{0,1:T(8,128)}, u32[]{:S(2)}) copy-start(f32[512,512]{0,1:T(8,128)} %get-tuple-element.23) | copy-start | bytes 3145732
  246.8 1.9 copy-start.2
where the time goes:
time: 255 us; the launch traced here: 252 us
  blocking collectives  140 us (55%)
  matrix products  86.6 us (34%)
  other arithmetic  13.9 us (5%)
  local copies, waits for them, and re-layouts  5.62 us (2%)
  between operations  5.04 us (2%)
    psum x1, blocking collectives, summed_grads(): total = lax.psum(partial_value, 'tok')  140 us
    dot_general x12, matrix products, newton_schulz(): jnp.dot(mixed, iterate, preferred_element_type=jnp.float32)  43 us
    dot_general x12, matrix products, newton_schulz(): jnp.dot(iterate, iterate.T, preferred_element_type=jnp.float32)  30 us
    unnamed x30, local copies, waits for them, and re-layouts  5.62 us

commit v1 on v0

v1 whole, which is shorter than its diff:
```python
import functools

import jax
import jax.numpy as jnp
from jax import lax
from jax.experimental import pallas as pl
from jax.experimental.pallas import tpu as pltpu
from jax.sharding import PartitionSpec as P

HEADS = 2
NS_STEPS = 2
CHUNKS = 4
MESH = pl.DeviceIdType.MESH
F32 = jnp.float32
BF16 = jnp.bfloat16


def dot(a, b):
    return jnp.dot(a, b, preferred_element_type=F32)


def dot_nt(a, b):
    return lax.dot_general(a, b, (((1,), (1,)), ((), ())), preferred_element_type=F32)


def dot_tn(a, b):
    return lax.dot_general(a, b, (((0,), (0,)), ((), ())), preferred_element_type=F32)


def kernel(
    Z, Y,
    k_ref, v_ref, q_ref, r_ref, w_ref,
    out_ref, neww_ref,
    o_loc, left, right, recv, sendbuf, m_buf, ss_buf, x_buf, g_buf, wn,
    tok_send, tok_recv, chain_send, chain_recv, w_send, w_recv, out_sem,
):
    tokens = k_ref.shape[0]
    D = w_ref.shape[2]
    R = D // CHUNKS
    PEERS = 2 * Y
    me = lax.axis_index("tok")
    c = me % 2
    y = (me // 2) % Y
    z = me // PEERS
    mine = y * 2 + c
    mid = Z // 2 - 1

    def at(zz, yy, cc):
        return {"tok": (zz * Y + yy) * 2 + cc}

    barrier = pltpu.get_barrier_semaphore()
    for d in range(1, PEERS):
        peer = z * PEERS + (mine + d) % PEERS
        pl.semaphore_signal(barrier, inc=1, device_id={"tok": peer}, device_id_type=MESH)

    @pl.when(z > 0)
    def _():
        pl.semaphore_signal(barrier, inc=1, device_id={"tok": me - PEERS}, device_id_type=MESH)

    @pl.when(z < Z - 1)
    def _():
        pl.semaphore_signal(barrier, inc=1, device_id={"tok": me + PEERS}, device_id_type=MESH)

    for h in range(HEADS):
        row = jnp.broadcast_to(r_ref[h : h + 1, :], (128, tokens))
        col = jnp.concatenate([row.T] * (D // 128), axis=1)
        o_loc[h] = (-col * v_ref[:, h * D : (h + 1) * D].astype(F32)).astype(BF16)

    own_rows = pl.ds(pl.multiple_of(mine * tokens, tokens), tokens)
    own_cols = pl.ds(pl.multiple_of(c * D, D), D)
    left[0, own_rows, :] = k_ref[:, own_cols]
    right[2, own_rows, :] = o_loc[c]

    pl.semaphore_wait(
        barrier, (PEERS - 1) + jnp.where(z > 0, 1, 0) + jnp.where(z < Z - 1, 1, 0)
    )

    def token_copies(d):
        p = (mine + d) % PEERS
        cc = p % 2
        dev = {"tok": z * PEERS + p}
        cols = pl.ds(pl.multiple_of(cc * D, D), D)
        return (
            pltpu.make_async_remote_copy(
                k_ref.at[:, cols], left.at[0, own_rows, :],
                tok_send.at[0, d - 1], tok_recv.at[0, d - 1],
                device_id=dev, device_id_type=MESH),
            pltpu.make_async_remote_copy(
                o_loc.at[cc], right.at[2, own_rows, :],
                tok_send.at[1, d - 1], tok_recv.at[1, d - 1],
                device_id=dev, device_id_type=MESH),
        )

    for d in range(1, PEERS):
        for cp in token_copies(d):
            cp.start()

    def forward_block(d, _):
        @pl.when(d > 0)
        def _():
            for cp in token_copies(d):
                cp.wait_recv()

        p = (mine + PEERS - d) % PEERS
        rows = pl.ds(pl.multiple_of(p * tokens, tokens), tokens)
        key = left[0, rows, :]
        gate = dot(key, w_ref[c, 0])
        upper = dot(key, w_ref[c, 1])
        back = dot_nt(right[2, rows, :], w_ref[c, 2])
        sigma = jax.nn.sigmoid(gate)
        silu_gate = gate * sigma
        left[1, rows, :] = (silu_gate * upper).astype(BF16)
        right[0, rows, :] = (back * upper * sigma * (1.0 + gate * (1.0 - sigma))).astype(BF16)
        right[1, rows, :] = (back * silu_gate).astype(BF16)
        return 0

    lax.fori_loop(0, PEERS, forward_block, 0)

    same = y == c
    w0 = jnp.where(y == 0, 0, jnp.where(c == 0, 2, 1))
    w1 = jnp.where(y == 0, 1, 2)
    own0 = jnp.where(same, 0, mid)
    own1 = Z - 1
    active0 = y < 2
    active1 = jnp.logical_and(same, y < 2)
    is_owner0 = jnp.logical_and(active0, z == own0)
    is_owner1 = jnp.logical_and(active1, z == own1)
    is_owner = jnp.logical_or(is_owner0, is_owner1)
    owned_w = jnp.where(is_owner1, w1, w0)

    def chain_copy(slot, i, step, side):
        return pltpu.make_async_remote_copy(
            sendbuf.at[slot, i], recv.at[side, slot, i],
            chain_send.at[slot, i], chain_recv.at[side, slot, i],
            device_id={"tok": me + step * PEERS}, device_id_type=MESH)

    def take(side, slot, i):
        chain_copy(slot, i, 1, side).wait_recv()
        part[...] += recv[side, slot, i].astype(F32)

    part = x_buf.at[0, pl.ds(0, R), :]

    def reduce_event(slot, i):
        w = jnp.where(slot == 0, w0, w1)
        own = jnp.where(slot == 0, own0, own1)
        cols = pl.ds(pl.multiple_of(i * R, R), R)
        part[...] = dot_tn(left[jnp.where(w == 2, 1, 0), :, cols], right[w])

        @pl.when(jnp.logical_and(z > 0, z <= own))
        def _():
            take(0, slot, i)

        @pl.when(jnp.logical_and(z < Z - 1, z >= own))
        def _():
            take(1, slot, i)

        @pl.when(z == own)
        def _():
            rounded = part[...].astype(BF16)
            m_buf[cols, :] = rounded
            wide = rounded.astype(F32)
            ss_buf[cols, :] = jnp.sum(wide * wide, axis=1, keepdims=True)

        @pl.when(z != own)
        def _():
            sendbuf[slot, i] = part[...].astype(BF16)

        @pl.when(z < own)
        def _():
            chain_copy(slot, i, 1, 0).start()

        @pl.when(z > own)
        def _():
            chain_copy(slot, i, -1, 1).start()

    near = jnp.where(z < Z // 2, 1, 0)
    first = jnp.where(active1, near, 0)
    lag = jnp.where(jnp.logical_or(z == 0, z == Z - 1), CHUNKS, 1)

    def reduce_step(t, _):
        @pl.when(t < CHUNKS)
        def _():
            reduce_event(first, t)

        @pl.when(jnp.logical_and(active1, jnp.logical_and(t >= lag, t < lag + CHUNKS)))
        def _():
            reduce_event(1 - first, t - lag)

        return 0

    @pl.when(active0)
    def _():
        lax.fori_loop(0, 2 * CHUNKS, reduce_step, 0)

    def place(w, h):
        col = jnp.where(w + h >= 2, 1, 0)
        own = jnp.where(
            col == h,
            jnp.where(w == h, 0, Z - 1),
            mid,
        )
        return col, own

    def w_copies(w, i, go):
        col, own = place(w, c)
        rows = pl.ds(pl.multiple_of(i * R, R), R)
        block = wn.at[c, w, rows, :]
        in_col = y == col

        def copy(kind, dev):
            cp = pltpu.make_async_remote_copy(
                block, block, w_send.at[w, i, kind], w_recv.at[c, w, i],
                device_id=dev, device_id_type=MESH)
            cp.start() if go else cp.wait_send()

        @pl.when(jnp.logical_and(in_col, jnp.logical_and(z >= own, z < Z - 1)))
        def _():
            copy(0, {"tok": me + PEERS})

        @pl.when(jnp.logical_and(in_col, jnp.logical_and(z <= own, z > 0)))
        def _():
            copy(1, {"tok": me - PEERS})

        @pl.when(in_col)
        def _():
            for dy in range(1, Y):
                copy(2 + dy, at(z, (y + dy) % Y, c))

        copy(2, at(z, y, 1 - c))

    def wait_block(h, w, i):
        rows = pl.ds(pl.multiple_of(i * R, R), R)
        block = wn.at[h, w, rows, :]
        pltpu.make_async_remote_copy(
            block, block, w_send.at[w, i, 2], w_recv.at[h, w, i],
            device_id=at(z, y, 1 - c), device_id_type=MESH).wait_recv()

    @pl.when(is_owner)
    def _():
        norm = jnp.sqrt(jnp.sum(ss_buf[...])) + 1e-07
        m_buf[...] = (m_buf[...].astype(F32) / norm).astype(BF16)
        for step in range(NS_STEPS):
            x = m_buf[...]
            g_buf[...] = dot_nt(x, x).astype(BF16)
            g = g_buf[...]
            mixed = (-4.775 * g.astype(F32) + 2.0315 * dot(g, g)).astype(BF16)
            x_buf[0] = 3.4445 * x.astype(F32) + dot(mixed, x)
            m_buf[...] = x_buf[0].astype(BF16)
        for i in range(CHUNKS):
            rows = slice(i * R, (i + 1) * R)
            old = w_ref[c, owned_w, rows, :].astype(F32)
            fresh = old - m_buf[rows, :].astype(F32)
            scale = jnp.sqrt(
                (jnp.mean(old * old, axis=1, keepdims=True) + 1e-06)
                / (jnp.mean(fresh * fresh, axis=1, keepdims=True) + 1e-06)
            )
            wn[c, owned_w, rows, :] = (fresh * scale).astype(BF16)
            w_copies(owned_w, i, True)

    def event(w, i, here):
        col, own = place(w, c)
        owner = jnp.logical_and(y == col, z == own)

        @pl.when(jnp.logical_and((y == col) == here, jnp.logical_not(owner)))
        def _():
            wait_block(c, w, i)
            w_copies(w, i, True)

    def spread(t, _):
        @pl.when(t < CHUNKS)
        def _():
            for w in range(3):
                event(jnp.where(z < Z // 2, w, 2 - w), t, True)

        @pl.when(t > 0)
        def _():
            for w in range(3):
                event(w, t - 1, False)

        return 0

    lax.fori_loop(0, CHUNKS + 1, spread, 0)

    def apply(h):
        cols = pl.ds(pl.multiple_of(h * D, D), D)
        query = q_ref[:, cols]
        gate = dot(query, wn[h, 0])
        upper = dot(query, wn[h, 1])
        hidden = (gate * jax.nn.sigmoid(gate) * upper).astype(BF16)
        out_ref[:, cols] = dot(hidden, wn[h, 2]).astype(BF16)

    def save(h, at_sem):
        return pltpu.make_async_copy(wn.at[h], neww_ref.at[h], out_sem.at[at_sem])

    save(c, 0).start()

    def turn(s, _):
        @pl.when(s == 1)
        def _():
            def wait_all(i, _):
                for w in range(3):
                    wait_block(1 - c, w, i)
                return 0

            lax.fori_loop(0, CHUNKS, wait_all, 0)
            save(1 - c, 1).start()

        apply(jnp.where(s == 0, c, 1 - c))
        return 0

    lax.fori_loop(0, 2, turn, 0)

    for d in range(1, PEERS):
        for cp in token_copies(d):
            cp.wait_send()

    def drain(i, _):
        @pl.when(jnp.logical_and(active0, z != own0))
        def _():
            chain_copy(0, i, 1, 0).wait_send()

        @pl.when(jnp.logical_and(active1, z != own1))
        def _():
            chain_copy(1, i, 1, 0).wait_send()

        for w in range(3):
            w_copies(w, i, False)
        return 0

    lax.fori_loop(0, CHUNKS, drain, 0)
    save(c, 0).wait()
    save(1 - c, 1).wait()


def body(Z, Y, keys, values, queries, rates, fast_weights):
    D = fast_weights.shape[2]
    tokens = keys.shape[0]
    rows = tokens * 2 * Y
    vmem = pl.BlockSpec(memory_space=pltpu.VMEM)

    def run(*refs):
        kernel(Z, Y, *refs)

    return pl.pallas_call(
        run,
        out_shape=(
            jax.ShapeDtypeStruct((tokens, HEADS * D), BF16),
            jax.ShapeDtypeStruct((HEADS, 3, D, D), BF16),
        ),
        in_specs=[vmem] * 5,
        out_specs=(vmem, pl.BlockSpec(memory_space=pl.ANY)),
        scratch_shapes=[
            pltpu.VMEM((HEADS, tokens, D), BF16),
            pltpu.VMEM((2, rows, D), BF16),
            pltpu.VMEM((3, rows, D), BF16),
            pltpu.VMEM((2, 2, CHUNKS, D // CHUNKS, D), BF16),
            pltpu.VMEM((2, CHUNKS, D // CHUNKS, D), BF16),
            pltpu.VMEM((D, D), BF16),
            pltpu.VMEM((D, 1), F32),
            pltpu.VMEM((1, D, D), F32),
            pltpu.VMEM((D, D), BF16),
            pltpu.VMEM((HEADS, 3, D, D), BF16),
            pltpu.SemaphoreType.DMA((2, 2 * Y - 1)),
            pltpu.SemaphoreType.DMA((2, 2 * Y - 1)),
            pltpu.SemaphoreType.DMA((2, CHUNKS)),
            pltpu.SemaphoreType.DMA((2, 2, CHUNKS)),
            pltpu.SemaphoreType.DMA((3, CHUNKS, 2 + Y)),
            pltpu.SemaphoreType.DMA((HEADS, 3, CHUNKS)),
            pltpu.SemaphoreType.DMA((2,)),
        ],
        compiler_params=pltpu.CompilerParams(
            collective_id=0, has_side_effects=True, vmem_limit_bytes=56 * 1024 * 1024
        ),
        name="ttt_step",
    )(keys, values, queries, rates, fast_weights)


def solution(mesh):
    chips = mesh.shape["tok"] // 2
    Y = 1
    while Y * Y * 4 <= chips and chips % (2 * Y) == 0:
        Y *= 2
    Z = chips // Y
    return jax.shard_map(
        functools.partial(body, Z, Y),
        mesh=mesh,
        in_specs=(
            P(("grp", "tok"), None),
            P(("grp", "tok"), None),
            P(("grp", "tok"), None),
            P(None, ("grp", "tok")),
            P(),
        ),
        out_specs=(P(("grp", "tok"), None), P("grp", None, None, None)),
        check_vma=False,
    )
```

time: 255 us -> 74.4 us (0.29); the launches traced: 252 us -> 74.2 us
  blocking collectives: 140 us -> 0 us
  matrix products: 86.6 us -> 0 us
  Pallas kernels: 0 us -> 68 us
  other arithmetic: 13.9 us -> 0 us
  between operations: 5.04 us -> 0.64 us
    psum x1 -> x0, blocking collectives: 140 us -> none  [summed_grads(): total = lax.psum(partial_value, 'tok')]
    dot_general x40 -> x0, matrix products: 86.6 us -> none  [the longest x12 43 us: newton_schulz(): jnp.dot(mixed, iterate, preferred_element_type=jnp.float32)]
    pallas_call x0 -> x1, Pallas kernels: none -> 68 us  [body(): pl.pallas_call(run, out_shape=(jax.ShapeDtypeStruct((tokens, HEADS * D),...]
    another operation x3 -> x0, other arithmetic: 4.07 us -> none  [the longest x2 3.95 us: swiglu_grads(): return jnp.stack([grad_gate, grad_upper, grad_down])]
    reduce_sum x2 -> x0, other arithmetic: 3.77 us -> none  [the longest x1 3.13 us: newton_schulz(): jnp.sum(wide * wide)]
    unnamed x5 -> x0, other arithmetic: 3.23 us -> none
    unnamed x30 -> x2, local copies, waits for them, and re-layouts: 5.62 us -> 5.61 us
where the time goes in v1:
time: 74.4 us; the launch traced here: 74.2 us
  Pallas kernels  68 us (91%)
  local copies, waits for them, and re-layouts  5.61 us (8%)
    pallas_call x1, Pallas kernels, body(): pl.pallas_call(run, out_shape=(jax.ShapeDtypeStruct((tokens, HEADS * D),...  68 us
    unnamed x2, local copies, waits for them, and re-layouts  5.61 us

profile of v1, /device:TPU:0, one launch (start us, length us, event | category | flops | bytes accessed | tf_op | source)
XLA Modules:
  0.0 74.2 jit_solution(14231847173616984346)
XLA Ops:
  0.6 68.0 %ttt_step.1 = (bf16[128,1024]{1,0:T(8,128)(2,1)}, bf16[2,3,512,512]{3,2,1,0:T(8,128)(2,1)}) custom-call(bf16[128,1024]{1,0:T(8,128)(2,1)} %refs_0_.1, bf16[128,1024]{1,0:T(8,128)(2,1)} %refs_1_.1, bf16[128,1024]{1,0:T(8,128)(2,1)} %refs_2_.1, f32[2,128]{1,0:T(2,128)} %refs_3_.1, bf16[2,3,512,512]{3,2,1,0:T(8,128)(2,1)} %refs_4_.1), custom_call_target="tpu_custom_call" | custom-call | tf_op jit(solution)/shard_map/ttt_step/pallas_call | solution.py:344
  68.6 1.7 %copy.9 = bf16[128,1024]{1,0:T(8,128)(2,1)} copy(bf16[128,1024]{1,0:T(8,128)(2,1)} %get-tuple-element.4) | data formatting | bytes 524288
  70.3 3.9 %copy.10 = bf16[2,3,512,512]{3,2,1,0:T(8,128)(2,1)} copy(bf16[2,3,512,512]{3,2,1,0:T(8,128)(2,1)} %get-tuple-element.5) | data formatting | bytes 6291456

commit v2 on v1

--- a/solution.py
+++ b/solution.py
@@ -9,7 +9,11 @@
 
 HEADS = 2
 NS_STEPS = 2
-CHUNKS = 4
+CHUNKS = 8
+SUM_CHUNKS = 4
+SUM_LAG = 2
+LAG = 3
+BOTH = 4
 MESH = pl.DeviceIdType.MESH
 F32 = jnp.float32
 BF16 = jnp.bfloat16
@@ -29,14 +33,16 @@
 
 def kernel(
     Z, Y,
-    k_ref, v_ref, q_ref, r_ref, w_ref,
+    k_hbm, v_hbm, q_hbm, r_hbm, w_hbm,
     out_ref, neww_ref,
+    v_ref, q_ref, r_ref, w_ref,
     o_loc, left, right, recv, sendbuf, m_buf, ss_buf, x_buf, g_buf, wn,
-    tok_send, tok_recv, chain_send, chain_recv, w_send, w_recv, out_sem,
+    tok_send, tok_recv, chain_send, chain_recv, w_send, w_recv, out_sem, in_sem,
 ):
-    tokens = k_ref.shape[0]
+    tokens = k_hbm.shape[0]
     D = w_ref.shape[2]
     R = D // CHUNKS
+    RS = D // SUM_CHUNKS
     PEERS = 2 * Y
     me = lax.axis_index("tok")
     c = me % 2
@@ -48,6 +54,18 @@
     def at(zz, yy, cc):
         return {"tok": (zz * Y + yy) * 2 + cc}
 
+    own_rows = pl.ds(pl.multiple_of(mine * tokens, tokens), tokens)
+    own_cols = pl.ds(pl.multiple_of(c * D, D), D)
+    loads = [
+        pltpu.make_async_copy(src, dst, in_sem.at[n])
+        for n, (src, dst) in enumerate((
+            (r_hbm, r_ref), (v_hbm, v_ref), (k_hbm.at[:, own_cols], left.at[0, own_rows, :]),
+            (w_hbm.at[c], w_ref.at[c]), (q_hbm, q_ref),
+        ))
+    ]
+    for load in loads:
+        load.start()
+
     barrier = pltpu.get_barrier_semaphore()
     for d in range(1, PEERS):
         peer = z * PEERS + (mine + d) % PEERS
@@ -61,14 +79,13 @@
     def _():
         pl.semaphore_signal(barrier, inc=1, device_id={"tok": me + PEERS}, device_id_type=MESH)
 
+    loads[0].wait()
+    loads[1].wait()
     for h in range(HEADS):
         row = jnp.broadcast_to(r_ref[h : h + 1, :], (128, tokens))
         col = jnp.concatenate([row.T] * (D // 128), axis=1)
         o_loc[h] = (-col * v_ref[:, h * D : (h + 1) * D].astype(F32)).astype(BF16)
 
-    own_rows = pl.ds(pl.multiple_of(mine * tokens, tokens), tokens)
-    own_cols = pl.ds(pl.multiple_of(c * D, D), D)
-    left[0, own_rows, :] = k_ref[:, own_cols]
     right[2, own_rows, :] = o_loc[c]
 
     pl.semaphore_wait(
@@ -82,7 +99,7 @@
         cols = pl.ds(pl.multiple_of(cc * D, D), D)
         return (
             pltpu.make_async_remote_copy(
-                k_ref.at[:, cols], left.at[0, own_rows, :],
+                k_hbm.at[:, cols], left.at[0, own_rows, :],
                 tok_send.at[0, d - 1], tok_recv.at[0, d - 1],
                 device_id=dev, device_id_type=MESH),
             pltpu.make_async_remote_copy(
@@ -94,6 +111,9 @@
     for d in range(1, PEERS):
         for cp in token_copies(d):
             cp.start()
+
+    loads[2].wait()
+    loads[3].wait()
 
     def forward_block(d, _):
         @pl.when(d > 0)
@@ -138,12 +158,12 @@
         chain_copy(slot, i, 1, side).wait_recv()
         part[...] += recv[side, slot, i].astype(F32)
 
-    part = x_buf.at[0, pl.ds(0, R), :]
+    part = x_buf.at[0, pl.ds(0, RS), :]
 
     def reduce_event(slot, i):
         w = jnp.where(slot == 0, w0, w1)
         own = jnp.where(slot == 0, own0, own1)
-        cols = pl.ds(pl.multiple_of(i * R, R), R)
+        cols = pl.ds(pl.multiple_of(i * RS, RS), RS)
         part[...] = dot_tn(left[jnp.where(w == 2, 1, 0), :, cols], right[w])
 
         @pl.when(jnp.logical_and(z > 0, z <= own))
@@ -173,24 +193,30 @@
         def _():
             chain_copy(slot, i, -1, 1).start()
 
+    def depth(own):
+        rise = jnp.where(z <= own, z, 0)
+        fall = jnp.where(z >= own, Z - 1 - z, 0)
+        return SUM_LAG * jnp.maximum(rise, fall)
+
     near = jnp.where(z < Z // 2, 1, 0)
     first = jnp.where(active1, near, 0)
-    lag = jnp.where(jnp.logical_or(z == 0, z == Z - 1), CHUNKS, 1)
+    lag_first = depth(jnp.where(first == 0, own0, own1))
+    lag_last = depth(jnp.where(first == 0, own1, own0))
 
     def reduce_step(t, _):
-        @pl.when(t < CHUNKS)
-        def _():
-            reduce_event(first, t)
-
-        @pl.when(jnp.logical_and(active1, jnp.logical_and(t >= lag, t < lag + CHUNKS)))
-        def _():
-            reduce_event(1 - first, t - lag)
+        @pl.when(jnp.logical_and(t >= lag_first, t < lag_first + SUM_CHUNKS))
+        def _():
+            reduce_event(first, t - lag_first)
+
+        @pl.when(jnp.logical_and(active1, jnp.logical_and(t >= lag_last, t < lag_last + SUM_CHUNKS)))
+        def _():
+            reduce_event(1 - first, t - lag_last)
 
         return 0
 
     @pl.when(active0)
     def _():
-        lax.fori_loop(0, 2 * CHUNKS, reduce_step, 0)
+        lax.fori_loop(0, SUM_CHUNKS + SUM_LAG * (Z - 1), reduce_step, 0)
 
     def place(w, h):
         col = jnp.where(w + h >= 2, 1, 0)
@@ -206,6 +232,8 @@
         rows = pl.ds(pl.multiple_of(i * R, R), R)
         block = wn.at[c, w, rows, :]
         in_col = y == col
+        both = i % BOTH == BOTH - 1
+        along = jnp.logical_or(in_col, both)
 
         def copy(kind, dev):
             cp = pltpu.make_async_remote_copy(
@@ -213,15 +241,15 @@
                 device_id=dev, device_id_type=MESH)
             cp.start() if go else cp.wait_send()
 
-        @pl.when(jnp.logical_and(in_col, jnp.logical_and(z >= own, z < Z - 1)))
+        @pl.when(jnp.logical_and(along, jnp.logical_and(z >= own, z < Z - 1)))
         def _():
             copy(0, {"tok": me + PEERS})
 
-        @pl.when(jnp.logical_and(in_col, jnp.logical_and(z <= own, z > 0)))
+        @pl.when(jnp.logical_and(along, jnp.logical_and(z <= own, z > 0)))
         def _():
             copy(1, {"tok": me - PEERS})
 
-        @pl.when(in_col)
+        @pl.when(jnp.logical_and(in_col, jnp.logical_or(jnp.logical_not(both), z == own)))
         def _():
             for dy in range(1, Y):
                 copy(2 + dy, at(z, (y + dy) % Y, c))
@@ -257,29 +285,21 @@
             wn[c, owned_w, rows, :] = (fresh * scale).astype(BF16)
             w_copies(owned_w, i, True)
 
-    def event(w, i, here):
-        col, own = place(w, c)
-        owner = jnp.logical_and(y == col, z == own)
-
-        @pl.when(jnp.logical_and((y == col) == here, jnp.logical_not(owner)))
-        def _():
-            wait_block(c, w, i)
-            w_copies(w, i, True)
-
     def spread(t, _):
-        @pl.when(t < CHUNKS)
-        def _():
-            for w in range(3):
-                event(jnp.where(z < Z // 2, w, 2 - w), t, True)
-
-        @pl.when(t > 0)
-        def _():
-            for w in range(3):
-                event(w, t - 1, False)
-
-        return 0
-
-    lax.fori_loop(0, CHUNKS + 1, spread, 0)
+        for n in range(3):
+            w = jnp.where(z < Z // 2, n, 2 - n)
+            col, own = place(w, c)
+            hops = jnp.abs(z - own) + jnp.where(y == col, 0, 1)
+            i = t - LAG * (hops - 1)
+
+            @pl.when(jnp.logical_and(hops > 0, jnp.logical_and(i >= 0, i < CHUNKS)))
+            def _():
+                wait_block(c, w, i)
+                w_copies(w, i, True)
+
+        return 0
+
+    lax.fori_loop(0, CHUNKS + LAG * (Z - 1), spread, 0)
 
     def apply(h):
         cols = pl.ds(pl.multiple_of(h * D, D), D)
@@ -308,21 +328,27 @@
         apply(jnp.where(s == 0, c, 1 - c))
         return 0
 
+    loads[4].wait()
     lax.fori_loop(0, 2, turn, 0)
 
     for d in range(1, PEERS):
         for cp in token_copies(d):
             cp.wait_send()
 
+    def drain_sums(i, _):
+        @pl.when(jnp.logical_and(active0, z != own0))
+        def _():
+            chain_copy(0, i, 1, 0).wait_send()
+
+        @pl.when(jnp.logical_and(active1, z != own1))
+        def _():
+            chain_copy(1, i, 1, 0).wait_send()
+
+        return 0
+
+    lax.fori_loop(0, SUM_CHUNKS, drain_sums, 0)
+
     def drain(i, _):
-        @pl.when(jnp.logical_and(active0, z != own0))
-        def _():
-            chain_copy(0, i, 1, 0).wait_send()
-
-        @pl.when(jnp.logical_and(active1, z != own1))
-        def _():
-            chain_copy(1, i, 1, 0).wait_send()
-
         for w in range(3):
             w_copies(w, i, False)
         return 0
@@ -330,6 +356,17 @@
     lax.fori_loop(0, CHUNKS, drain, 0)
     save(c, 0).wait()
     save(1 - c, 1).wait()
+
+
+def store(a_ref, b_ref, a_out, b_out, sem):
+    copies = [
+        pltpu.make_async_copy(b_ref, b_out, sem.at[0]),
+        pltpu.make_async_copy(a_ref, a_out, sem.at[1]),
+    ]
+    for cp in copies:
+        cp.start()
+    for cp in copies:
+        cp.wait()
 
 
 def body(Z, Y, keys, values, queries, rates, fast_weights):
@@ -337,24 +374,29 @@
     tokens = keys.shape[0]
     rows = tokens * 2 * Y
     vmem = pl.BlockSpec(memory_space=pltpu.VMEM)
+    hbm = pl.BlockSpec(memory_space=pltpu.MemorySpace.HBM)
 
     def run(*refs):
         kernel(Z, Y, *refs)
 
-    return pl.pallas_call(
+    out, fresh = pl.pallas_call(
         run,
         out_shape=(
             jax.ShapeDtypeStruct((tokens, HEADS * D), BF16),
             jax.ShapeDtypeStruct((HEADS, 3, D, D), BF16),
         ),
-        in_specs=[vmem] * 5,
+        in_specs=[hbm] * 5,
         out_specs=(vmem, pl.BlockSpec(memory_space=pl.ANY)),
         scratch_shapes=[
+            pltpu.VMEM((tokens, HEADS * D), BF16),
+            pltpu.VMEM((tokens, HEADS * D), BF16),
+            pltpu.VMEM(rates.shape, F32),
+            pltpu.VMEM((HEADS, 3, D, D), BF16),
             pltpu.VMEM((HEADS, tokens, D), BF16),
             pltpu.VMEM((2, rows, D), BF16),
             pltpu.VMEM((3, rows, D), BF16),
-            pltpu.VMEM((2, 2, CHUNKS, D // CHUNKS, D), BF16),
-            pltpu.VMEM((2, CHUNKS, D // CHUNKS, D), BF16),
+            pltpu.VMEM((2, 2, SUM_CHUNKS, D // SUM_CHUNKS, D), BF16),
+            pltpu.VMEM((2, SUM_CHUNKS, D // SUM_CHUNKS, D), BF16),
             pltpu.VMEM((D, D), BF16),
             pltpu.VMEM((D, 1), F32),
             pltpu.VMEM((1, D, D), F32),
@@ -362,17 +404,31 @@
             pltpu.VMEM((HEADS, 3, D, D), BF16),
             pltpu.SemaphoreType.DMA((2, 2 * Y - 1)),
             pltpu.SemaphoreType.DMA((2, 2 * Y - 1)),
-            pltpu.SemaphoreType.DMA((2, CHUNKS)),
-            pltpu.SemaphoreType.DMA((2, 2, CHUNKS)),
+            pltpu.SemaphoreType.DMA((2, SUM_CHUNKS)),
+            pltpu.SemaphoreType.DMA((2, 2, SUM_CHUNKS)),
             pltpu.SemaphoreType.DMA((3, CHUNKS, 2 + Y)),
             pltpu.SemaphoreType.DMA((HEADS, 3, CHUNKS)),
             pltpu.SemaphoreType.DMA((2,)),
+            pltpu.SemaphoreType.DMA((5,)),
         ],
         compiler_params=pltpu.CompilerParams(
-            collective_id=0, has_side_effects=True, vmem_limit_bytes=56 * 1024 * 1024
+            collective_id=0, has_side_effects=True, vmem_limit_bytes=30 * 1024 * 1024
         ),
         name="ttt_step",
-    )(keys, values, queries, rates, fast_weights)
+    )(*[pltpu.with_memory_space_constraint(a, pltpu.MemorySpace.HBM) for a in (keys, values, queries, rates, fast_weights)])
+    anywhere = pl.BlockSpec(memory_space=pl.ANY)
+    return pl.pallas_call(
+        store,
+        out_shape=(
+            jax.ShapeDtypeStruct(out.shape, BF16),
+            jax.ShapeDtypeStruct(fresh.shape, BF16),
+        ),
+        in_specs=[anywhere] * 2,
+        out_specs=(hbm, hbm),
+        scratch_shapes=[pltpu.SemaphoreType.DMA((2,))],
+        compiler_params=pltpu.CompilerParams(vmem_limit_bytes=1024 * 1024),
+        name="store",
+    )(out, fresh)
 
 
 def solution(mesh):

time: 74.4 us -> 62.6 us (0.84)
  Pallas kernels: 68 us -> 61.8 us
  local copies, waits for them, and re-layouts: 5.61 us -> 0 us
    pallas_call x1, Pallas kernels: 68 us -> 60.1 us  [body(): pl.pallas_call(run, out_shape=(jax.ShapeDtypeStruct((tokens, HEADS * D),...]
    unnamed x2 -> x0, local copies, waits for them, and re-layouts: 5.61 us -> none
    pallas_call x0 -> x1, Pallas kernels: none -> 1.76 us  [body(): pl.pallas_call(store, out_shape=(jax.ShapeDtypeStruct(out.shape, BF16), j...]
where the time goes in v2:
time: 62.6 us; the launch traced here: 62.5 us
  Pallas kernels  61.8 us (99%)
  between operations  0.64 us (1%)
    pallas_call x1, Pallas kernels, body(): pl.pallas_call(run, out_shape=(jax.ShapeDtypeStruct((tokens, HEADS * D),...  60.1 us
    pallas_call x1, Pallas kernels, body(): pl.pallas_call(store, out_shape=(jax.ShapeDtypeStruct(out.shape, BF16), j...  1.76 us

profile of v2, /device:TPU:0, one launch (start us, length us, event | category | flops | bytes accessed | tf_op | source)
XLA Modules:
  0.0 62.5 jit_solution(15671768772483448818)
XLA Ops:
  0.6 60.1 %ttt_step.1 = (bf16[128,1024]{1,0:T(8,128)(2,1)S(1)}, bf16[2,3,512,512]{3,2,1,0:T(8,128)(2,1)S(1)}) custom-call(bf16[128,1024]{1,0:T(8,128)(2,1)} %refs_0_.1, bf16[128,1024]{1,0:T(8,128)(2,1)} %refs_1_.1, bf16[128,1024]{1,0:T(8,128)(2,1)} %refs_2_.1, f32[2,128]{1,0:T(2,128)} %refs_3_.1, bf16[2,3,512,512]{3,2,1,0:T(8,128)(2,1)} %refs_4_.1), custom_call_target="tpu_custom_call" | custom-call | tf_op jit(solution)/shard_map/ttt_step/pallas_call | solution.py:382
  60.7 1.8 %store.1 = (bf16[128,1024]{1,0:T(8,128)(2,1)}, bf16[2,3,512,512]{3,2,1,0:T(8,128)(2,1)}) custom-call(bf16[128,1024]{1,0:T(8,128)(2,1)S(1)} %get-tuple-element.4.a_ref, bf16[2,3,512,512]{3,2,1,0:T(8,128)(2,1)S(1)} %get-tuple-element.5.b_ref), custom_call_target="tpu_custom_call" | custom-call | tf_op jit(solution)/shard_map/store/pallas_call | solution.py:420

commit v3 on v2

--- a/solution.py
+++ b/solution.py
@@ -10,10 +10,13 @@
 HEADS = 2
 NS_STEPS = 2
 CHUNKS = 8
-SUM_CHUNKS = 4
-SUM_LAG = 2
-LAG = 3
+SUM_CHUNKS = 8
+HALVES = 2
+CROSS = 2
+SUM_LAG = 3
+LAG = 4
 BOTH = 4
+SHIFT = 0
 MESH = pl.DeviceIdType.MESH
 F32 = jnp.float32
 BF16 = jnp.bfloat16
@@ -36,13 +39,14 @@
     k_hbm, v_hbm, q_hbm, r_hbm, w_hbm,
     out_ref, neww_ref,
     v_ref, q_ref, r_ref, w_ref,
-    o_loc, left, right, recv, sendbuf, m_buf, ss_buf, x_buf, g_buf, wn,
-    tok_send, tok_recv, chain_send, chain_recv, w_send, w_recv, out_sem, in_sem,
+    o_loc, left, right, recv, sendbuf, m_buf, x_buf, g_buf, wn, recv_y,
+    tok_send, tok_recv, chain_send, chain_recv, cross_recv, w_send, w_recv, out_sem, in_sem,
 ):
     tokens = k_hbm.shape[0]
     D = w_ref.shape[2]
     R = D // CHUNKS
-    RS = D // SUM_CHUNKS
+    RS = D * HALVES // SUM_CHUNKS
+    CS = D // HALVES
     PEERS = 2 * Y
     me = lax.axis_index("tok")
     c = me % 2
@@ -108,20 +112,35 @@
                 device_id=dev, device_id_type=MESH),
         )
 
+    def reached(d):
+        p = (mine + d) % PEERS
+        return jnp.logical_or(p % 2 != CROSS, p // 2 == y)
+
     for d in range(1, PEERS):
-        for cp in token_copies(d):
-            cp.start()
+
+        @pl.when(reached(d))
+        def _():
+            for cp in token_copies(d):
+                cp.start()
 
     loads[2].wait()
     loads[3].wait()
 
     def forward_block(d, _):
+        p = (mine + PEERS - d) % PEERS
+
+        @pl.when(jnp.logical_or(c != CROSS, p // 2 == y))
+        def _():
+            forward_rows(d, p)
+
+        return 0
+
+    def forward_rows(d, p):
         @pl.when(d > 0)
         def _():
             for cp in token_copies(d):
                 cp.wait_recv()
 
-        p = (mine + PEERS - d) % PEERS
         rows = pl.ds(pl.multiple_of(p * tokens, tokens), tokens)
         key = left[0, rows, :]
         gate = dot(key, w_ref[c, 0])
@@ -132,100 +151,116 @@
         left[1, rows, :] = (silu_gate * upper).astype(BF16)
         right[0, rows, :] = (back * upper * sigma * (1.0 + gate * (1.0 - sigma))).astype(BF16)
         right[1, rows, :] = (back * silu_gate).astype(BF16)
-        return 0
 
     lax.fori_loop(0, PEERS, forward_block, 0)
-
-    same = y == c
-    w0 = jnp.where(y == 0, 0, jnp.where(c == 0, 2, 1))
-    w1 = jnp.where(y == 0, 1, 2)
-    own0 = jnp.where(same, 0, mid)
-    own1 = Z - 1
-    active0 = y < 2
-    active1 = jnp.logical_and(same, y < 2)
-    is_owner0 = jnp.logical_and(active0, z == own0)
-    is_owner1 = jnp.logical_and(active1, z == own1)
-    is_owner = jnp.logical_or(is_owner0, is_owner1)
-    owned_w = jnp.where(is_owner1, w1, w0)
-
-    def chain_copy(slot, i, step, side):
-        return pltpu.make_async_remote_copy(
-            sendbuf.at[slot, i], recv.at[side, slot, i],
-            chain_send.at[slot, i], chain_recv.at[side, slot, i],
-            device_id={"tok": me + step * PEERS}, device_id_type=MESH)
-
-    def take(side, slot, i):
-        chain_copy(slot, i, 1, side).wait_recv()
-        part[...] += recv[side, slot, i].astype(F32)
-
-    part = x_buf.at[0, pl.ds(0, RS), :]
-
-    def reduce_event(slot, i):
-        w = jnp.where(slot == 0, w0, w1)
-        own = jnp.where(slot == 0, own0, own1)
-        cols = pl.ds(pl.multiple_of(i * RS, RS), RS)
-        part[...] = dot_tn(left[jnp.where(w == 2, 1, 0), :, cols], right[w])
-
-        @pl.when(jnp.logical_and(z > 0, z <= own))
-        def _():
-            take(0, slot, i)
-
-        @pl.when(jnp.logical_and(z < Z - 1, z >= own))
-        def _():
-            take(1, slot, i)
-
-        @pl.when(z == own)
-        def _():
-            rounded = part[...].astype(BF16)
-            m_buf[cols, :] = rounded
-            wide = rounded.astype(F32)
-            ss_buf[cols, :] = jnp.sum(wide * wide, axis=1, keepdims=True)
-
-        @pl.when(z != own)
-        def _():
-            sendbuf[slot, i] = part[...].astype(BF16)
-
-        @pl.when(z < own)
-        def _():
-            chain_copy(slot, i, 1, 0).start()
-
-        @pl.when(z > own)
-        def _():
-            chain_copy(slot, i, -1, 1).start()
-
-    def depth(own):
-        rise = jnp.where(z <= own, z, 0)
-        fall = jnp.where(z >= own, Z - 1 - z, 0)
-        return SUM_LAG * jnp.maximum(rise, fall)
-
-    near = jnp.where(z < Z // 2, 1, 0)
-    first = jnp.where(active1, near, 0)
-    lag_first = depth(jnp.where(first == 0, own0, own1))
-    lag_last = depth(jnp.where(first == 0, own1, own0))
-
-    def reduce_step(t, _):
-        @pl.when(jnp.logical_and(t >= lag_first, t < lag_first + SUM_CHUNKS))
-        def _():
-            reduce_event(first, t - lag_first)
-
-        @pl.when(jnp.logical_and(active1, jnp.logical_and(t >= lag_last, t < lag_last + SUM_CHUNKS)))
-        def _():
-            reduce_event(1 - first, t - lag_last)
-
-        return 0
-
-    @pl.when(active0)
-    def _():
-        lax.fori_loop(0, SUM_CHUNKS + SUM_LAG * (Z - 1), reduce_step, 0)
 
     def place(w, h):
         col = jnp.where(w + h >= 2, 1, 0)
         own = jnp.where(
             col == h,
             jnp.where(w == h, 0, Z - 1),
-            mid,
+            mid + SHIFT * col,
         )
         return col, own
+
+    def crosses(w):
+        return jnp.logical_and(c == CROSS, y != place(w, c)[0])
+
+    def active(w):
+        return jnp.logical_or(c == CROSS, y == place(w, c)[0])
+
+    def owns(w):
+        col, own = place(w, c)
+        return jnp.logical_and(y == col, z == own)
+
+    is_owner = functools.reduce(jnp.logical_or, [owns(w) for w in range(3)])
+    owned_w = jnp.where(owns(0), 0, jnp.where(owns(1), 1, 2))
+
+    def chain_copy(w, i, step, side):
+        return pltpu.make_async_remote_copy(
+            sendbuf.at[w, i], recv.at[side, w, i],
+            chain_send.at[w, i], chain_recv.at[side, w, i],
+            device_id={"tok": me + step * PEERS}, device_id_type=MESH)
+
+    def cross_copy(w, i, slot):
+        return pltpu.make_async_remote_copy(
+            sendbuf.at[w, i], recv_y.at[slot, i],
+            chain_send.at[w, i], cross_recv.at[slot, i],
+            device_id=at(z, place(w, c)[0], c), device_id_type=MESH)
+
+    def take(side, w, i):
+        chain_copy(w, i, 1, side).wait_recv()
+        part[...] += recv[side, w, i].astype(F32)
+
+    part = x_buf.at[0, pl.ds(0, RS), pl.ds(0, CS)]
+    chip_rows = pl.ds(pl.multiple_of(y * 2 * tokens, 2 * tokens), 2 * tokens)
+
+    def reduce_event(w, i):
+        col, own = place(w, c)
+        rows = pl.ds(pl.multiple_of((i // HALVES) * RS, RS), RS)
+        cols = pl.ds(pl.multiple_of((i % HALVES) * CS, CS), CS)
+        side_l = 1 if w == 2 else 0
+
+        @pl.when(c != CROSS)
+        def _():
+            part[...] = dot_tn(left[side_l, :, rows], right[w, :, cols])
+
+        @pl.when(c == CROSS)
+        def _():
+            part[...] = dot_tn(left[side_l, chip_rows, rows], right[w, chip_rows, cols])
+
+        @pl.when(jnp.logical_and(z > 0, z <= own))
+        def _():
+            take(0, w, i)
+
+        @pl.when(jnp.logical_and(z < Z - 1, z >= own))
+        def _():
+            take(1, w, i)
+
+        @pl.when(owns(w))
+        def _():
+            @pl.when(c == CROSS)
+            def _():
+                for slot in range(Y - 1):
+                    cross_copy(w, i, slot).wait_recv()
+                    part[...] += recv_y[slot, i].astype(F32)
+
+            m_buf[rows, cols] = part[...].astype(BF16)
+
+        @pl.when(jnp.logical_not(owns(w)))
+        def _():
+            sendbuf[w, i] = part[...].astype(BF16)
+
+        @pl.when(z < own)
+        def _():
+            chain_copy(w, i, 1, 0).start()
+
+        @pl.when(z > own)
+        def _():
+            chain_copy(w, i, -1, 1).start()
+
+        @pl.when(jnp.logical_and(z == own, crosses(w)))
+        def _():
+            cross_copy(w, i, (y + Y - col) % Y - 1).start()
+
+    def depth(w):
+        own = place(w, c)[1]
+        rise = jnp.where(z <= own, z, 0)
+        fall = jnp.where(z >= own, Z - 1 - z, 0)
+        met = jnp.where(jnp.logical_and(owns(w), c == CROSS), 1, 0)
+        return SUM_LAG * (jnp.maximum(rise, fall) + met)
+
+    def reduce_step(t, _):
+        for w in range(3):
+            i = t - depth(w)
+
+            @pl.when(jnp.logical_and(active(w), jnp.logical_and(i >= 0, i < SUM_CHUNKS)))
+            def _():
+                reduce_event(w, i)
+
+        return 0
+
+    lax.fori_loop(0, SUM_CHUNKS + SUM_LAG * Z, reduce_step, 0)
 
     def w_copies(w, i, go):
         col, own = place(w, c)
@@ -265,8 +300,9 @@
 
     @pl.when(is_owner)
     def _():
-        norm = jnp.sqrt(jnp.sum(ss_buf[...])) + 1e-07
-        m_buf[...] = (m_buf[...].astype(F32) / norm).astype(BF16)
+        wide = m_buf[...].astype(F32)
+        norm = jnp.sqrt(jnp.sum(wide * wide)) + 1e-07
+        m_buf[...] = (wide / norm).astype(BF16)
         for step in range(NS_STEPS):
             x = m_buf[...]
             g_buf[...] = dot_nt(x, x).astype(BF16)
@@ -332,17 +368,18 @@
     lax.fori_loop(0, 2, turn, 0)
 
     for d in range(1, PEERS):
-        for cp in token_copies(d):
-            cp.wait_send()
+
+        @pl.when(reached(d))
+        def _():
+            for cp in token_copies(d):
+                cp.wait_send()
 
     def drain_sums(i, _):
-        @pl.when(jnp.logical_and(active0, z != own0))
-        def _():
-            chain_copy(0, i, 1, 0).wait_send()
-
-        @pl.when(jnp.logical_and(active1, z != own1))
-        def _():
-            chain_copy(1, i, 1, 0).wait_send()
+        for w in range(3):
+
+            @pl.when(jnp.logical_and(active(w), jnp.logical_not(owns(w))))
+            def _():
+                chain_copy(w, i, 1, 0).wait_send()
 
         return 0
 
@@ -395,17 +432,18 @@
             pltpu.VMEM((HEADS, tokens, D), BF16),
             pltpu.VMEM((2, rows, D), BF16),
             pltpu.VMEM((3, rows, D), BF16),
-            pltpu.VMEM((2, 2, SUM_CHUNKS, D // SUM_CHUNKS, D), BF16),
-            pltpu.VMEM((2, SUM_CHUNKS, D // SUM_CHUNKS, D), BF16),
+            pltpu.VMEM((2, 3, SUM_CHUNKS, D * HALVES // SUM_CHUNKS, D // HALVES), BF16),
+            pltpu.VMEM((3, SUM_CHUNKS, D * HALVES // SUM_CHUNKS, D // HALVES), BF16),
             pltpu.VMEM((D, D), BF16),
-            pltpu.VMEM((D, 1), F32),
             pltpu.VMEM((1, D, D), F32),
             pltpu.VMEM((D, D), BF16),
             pltpu.VMEM((HEADS, 3, D, D), BF16),
+            pltpu.VMEM((Y - 1, SUM_CHUNKS, D * HALVES // SUM_CHUNKS, D // HALVES), BF16),
             pltpu.SemaphoreType.DMA((2, 2 * Y - 1)),
             pltpu.SemaphoreType.DMA((2, 2 * Y - 1)),
-            pltpu.SemaphoreType.DMA((2, SUM_CHUNKS)),
-            pltpu.SemaphoreType.DMA((2, 2, SUM_CHUNKS)),
+            pltpu.SemaphoreType.DMA((3, SUM_CHUNKS)),
+            pltpu.SemaphoreType.DMA((2, 3, SUM_CHUNKS)),
+            pltpu.SemaphoreType.DMA((Y - 1, SUM_CHUNKS)),
             pltpu.SemaphoreType.DMA((3, CHUNKS, 2 + Y)),
             pltpu.SemaphoreType.DMA((HEADS, 3, CHUNKS)),
             pltpu.SemaphoreType.DMA((2,)),

time: 62.6 us -> 62.1 us (level)
  Pallas kernels: 61.8 us -> 61.1 us
    pallas_call x1, Pallas kernels: 60.1 us -> 59.4 us  [body(): pl.pallas_call(run, out_shape=(jax.ShapeDtypeStruct((tokens, HEADS * D),...]
where the time goes in v3:
time: 62.1 us; the launch traced here: 61.8 us
  Pallas kernels  61.1 us (98%)
  between operations  0.64 us (1%)
    pallas_call x1, Pallas kernels, body(): pl.pallas_call(run, out_shape=(jax.ShapeDtypeStruct((tokens, HEADS * D),...  59.4 us
    pallas_call x1, Pallas kernels, body(): pl.pallas_call(store, out_shape=(jax.ShapeDtypeStruct(out.shape, BF16), j...  1.76 us

profile of v3, /device:TPU:0, one launch (start us, length us, event | category | flops | bytes accessed | tf_op | source)
XLA Modules:
  0.0 61.8 jit_solution(9811598124246910274)
XLA Ops:
  0.6 59.4 %ttt_step.1 = (bf16[128,1024]{1,0:T(8,128)(2,1)S(1)}, bf16[2,3,512,512]{3,2,1,0:T(8,128)(2,1)S(1)}) custom-call(bf16[128,1024]{1,0:T(8,128)(2,1)} %refs_0_.1, bf16[128,1024]{1,0:T(8,128)(2,1)} %refs_1_.1, bf16[128,1024]{1,0:T(8,128)(2,1)} %refs_2_.1, f32[2,128]{1,0:T(2,128)} %refs_3_.1, bf16[2,3,512,512]{3,2,1,0:T(8,128)(2,1)} %refs_4_.1), custom_call_target="tpu_custom_call" | custom-call | tf_op jit(solution)/shard_map/ttt_step/pallas_call | solution.py:419
  60.0 1.8 %store.1 = (bf16[128,1024]{1,0:T(8,128)(2,1)}, bf16[2,3,512,512]{3,2,1,0:T(8,128)(2,1)}) custom-call(bf16[128,1024]{1,0:T(8,128)(2,1)S(1)} %get-tuple-element.4.a_ref, bf16[2,3,512,512]{3,2,1,0:T(8,128)(2,1)S(1)} %get-tuple-element.5.b_ref), custom_call_target="tpu_custom_call" | custom-call | tf_op jit(solution)/shard_map/store/pallas_call | solution.py:458
